TPU v7x, 32 devices: a whole 2x2x4 slice. The times are simulated.
32 devices in a mesh: dp: 8 (over z, y), tensor: 4 (over x, core).
Axes of the slice: x: 2, y: 2, z: 4, core: 2. Of those that a mesh axis runs over, the one named last changes fastest.
Arguments:
- inputs: bfloat16 [4096, 768], P(('dp', 'tensor')), may hold values from -6 to 6
- prev_logits: bfloat16 [4096, 12, 4096], P('dp', 'tensor'), may hold values from -6 to 6
- w_query: bfloat16 [768, 768], P('dp', 'tensor'), may hold values from -0.21875 to 0.21875
- w_key: bfloat16 [768, 768], P('dp', 'tensor'), may hold values from -0.21875 to 0.21875
- w_value: bfloat16 [768, 768], P('dp', 'tensor'), may hold values from -0.21875 to 0.21875
- w_attn_out: bfloat16 [768, 768], P('tensor', 'dp'), may hold values from -2.5 to 2.5
- w_ffn_in: bfloat16 [768, 3072], P('dp', 'tensor'), may hold values from -0.21875 to 0.21875
- ffn_bias: bfloat16 [3072], P(('tensor', 'dp')), may hold values from -3 to 3
- w_ffn_out: bfloat16 [3072, 768], P(('tensor', 'dp')), may hold values from -0.109375 to 0.109375
- norm1_gain: float32 [768], replicated, may hold values from 0.5 to 1.5
- norm1_shift: float32 [768], replicated, may hold values from -2 to 2
- norm2_gain: float32 [768], replicated, may hold values from 0.5 to 1.5
- norm2_shift: float32 [768], replicated, may hold values from -2 to 2
- token_segment: int32 [4096], replicated, may hold values from 0 to 12, as said below
- segment_parent: int32 [1, 13], replicated, may hold values from 0 to 4, as said below
- out_grad: bfloat16 [4096, 768], P(('dp', 'tensor')), may hold values from -6 to 6
- logit_grad: bfloat16 [4096, 12, 4096], P('dp', 'tensor'), may hold values from -6 to 6
Outputs:
- output: bfloat16 [4096, 768], P(('dp', 'tensor'))
- logits: bfloat16 [4096, 12, 4096], P('dp', 'tensor')
- input_grad: float32 [4096, 768], P(('dp', 'tensor'))
- prev_grad: bfloat16 [4096, 12, 4096], P('dp', 'tensor')
- w_query_grad: float32 [768, 768], P('dp', 'tensor')
- w_key_grad: float32 [768, 768], P('dp', 'tensor')
- w_value_grad: float32 [768, 768], P('dp', 'tensor')
- w_attn_out_grad: float32 [768, 768], P('tensor', 'dp')
- w_ffn_in_grad: float32 [768, 3072], P('dp', 'tensor')
- ffn_bias_grad: float32 [3072], P(('tensor', 'dp'))
- w_ffn_out_grad: float32 [3072, 768], P(('tensor', 'dp'))
- norm1_gain_grad: float32 [768], replicated
- norm1_shift_grad: float32 [768], replicated
- norm2_gain_grad: float32 [768], replicated
- norm2_shift_grad: float32 [768], replicated
Inputs may be any that keep to these rules, and one draw needn't show every extreme that they name: `token_segment`: in each tree the first 2048 tokens are segment 0, the trunk; the other tokens hold the 4 branches (segments 1 to 4, 256 tokens each) and the 8 leaves (segments 5 to 12, 128 tokens each), each segment one contiguous run, in an order that varies from tree to tree. `segment_parent`: row t lists the parents of tree t's segments: 0 for the trunk and every branch, a branch for every leaf, each branch the parent of exactly two leaves.
All inputs are finite; a program needn't handle non-finite values.
Results may differ from a plain program's by a relative error of at most 0.017.
Values may be sent and summed in bfloat16 or wider, within the bound.
No kernel may reach another device: no remote copies, remote signals or barrier semaphores. Data moves between devices by JAX's collectives and lax.ppermute only.
A program may use at most 256 MiB of HBM per device.

v0:
```python
import jax
import jax.numpy as jnp
from jax import lax
from jax.sharding import PartitionSpec as P

E = 64
EPSILON = 1e-12


def layer_norm(values, norm_gain, norm_shift):
    center = values - jnp.mean(values, axis=-1, keepdims=True)
    spread = jnp.mean(center * center, axis=-1, keepdims=True)
    return center * lax.rsqrt(spread + EPSILON) * norm_gain + norm_shift


def gelu_exact(values):
    return jax.nn.gelu(values, approximate=False)


def attend_forward(key_count, local_heads, head_dim, score_scale):
    columns = local_heads * head_dim

    def run(operands):
        query_heads, tree_kv, previous, allowed = operands
        group_rows = query_heads.shape[0]
        key_heads = tree_kv[:key_count, :columns].reshape(key_count, local_heads, head_dim)
        value_heads = tree_kv[:key_count, columns:].reshape(key_count, local_heads, head_dim)
        scores = jnp.einsum(
            "qhe,khe->qhk", query_heads, key_heads, preferred_element_type=jnp.float32
        ) * score_scale + previous.astype(jnp.float32)
        logits = jnp.where(allowed, scores, 0.0).astype(jnp.bfloat16)
        masked = jnp.where(allowed, scores, -jnp.inf)
        row_max = jnp.max(masked, axis=-1, keepdims=True)
        exponent = jnp.exp(masked - row_max)
        row_total = jnp.sum(exponent, axis=-1, keepdims=True)
        log_total = row_max + jnp.log(row_total)
        weights = (exponent / row_total).astype(jnp.bfloat16)
        mixed = (
            jnp.einsum("qhk,khe->qhe", weights, value_heads, preferred_element_type=jnp.float32)
            .astype(jnp.bfloat16)
            .reshape(group_rows, columns)
        )
        return (mixed, logits, log_total)

    return run


def attend_backward(key_count, local_heads, head_dim, score_scale):
    columns = local_heads * head_dim

    def run(operands):
        query_heads, tree_kv, previous, allowed, log_total, grad_mixed_heads, upstream = operands
        group_rows = query_heads.shape[0]
        key_heads = tree_kv[:key_count, :columns].reshape(key_count, local_heads, head_dim)
        value_heads = tree_kv[:key_count, columns:].reshape(key_count, local_heads, head_dim)
        scores = jnp.einsum(
            "qhe,khe->qhk", query_heads, key_heads, preferred_element_type=jnp.float32
        ) * score_scale + previous.astype(jnp.float32)
        attention_weight = jnp.exp(jnp.where(allowed, scores, -jnp.inf) - log_total)
        grad_weight = jnp.einsum(
            "qhe,khe->qhk", grad_mixed_heads, value_heads, preferred_element_type=jnp.float32
        )
        grad_values = jnp.einsum(
            "qhk,qhe->khe",
            attention_weight.astype(jnp.bfloat16),
            grad_mixed_heads,
            preferred_element_type=jnp.float32,
        )
        grad_soft = attention_weight * (
            grad_weight - jnp.sum(attention_weight * grad_weight, axis=-1, keepdims=True)
        )
        grad_scores = jnp.where(allowed, upstream.astype(jnp.float32) + grad_soft, 0.0).astype(
            jnp.bfloat16
        )
        grad_query = (
            (
                jnp.einsum(
                    "qhk,khe->qhe", grad_scores, key_heads, preferred_element_type=jnp.float32
                )
                * score_scale
            )
            .astype(jnp.bfloat16)
            .reshape(group_rows, columns)
        )
        grad_keys = (
            jnp.einsum("qhk,qhe->khe", grad_scores, query_heads, preferred_element_type=jnp.float32)
            * score_scale
        )
        tree_grads = jnp.concatenate(
            [grad_keys.reshape(key_count, columns), grad_values.reshape(key_count, columns)], axis=1
        )
        return (grad_scores, grad_query, tree_grads)

    return run


def shards(
    inputs,
    prev_logits,
    w_query,
    w_key,
    w_value,
    w_attn_out,
    w_ffn_in,
    ffn_bias,
    w_ffn_out,
    norm1_gain,
    norm1_shift,
    norm2_gain,
    norm2_shift,
    token_segment,
    segment_parent,
    out_grad,
    logit_grad,
):
    group_rows = prev_logits.shape[0]
    local_heads = prev_logits.shape[1]
    tree_len = prev_logits.shape[2]
    head_dim = E
    columns = local_heads * head_dim
    spread = tree_len // group_rows
    score_scale = head_dim ** (-0.5)
    data_index = lax.axis_index("dp")
    tree_index = data_index // spread
    local_index = data_index % spread
    query_start = local_index * group_rows
    full_query, full_key, full_value, full_attn, full_inner, full_bias, full_outer = (
        lax.all_gather(w_query, "dp", axis=0, tiled=True),
        lax.all_gather(w_key, "dp", axis=0, tiled=True),
        lax.all_gather(w_value, "dp", axis=0, tiled=True),
        lax.all_gather(w_attn_out, "dp", axis=1, tiled=True),
        lax.all_gather(w_ffn_in, "dp", axis=0, tiled=True),
        lax.all_gather(ffn_bias, "dp", axis=0, tiled=True),
        lax.all_gather(w_ffn_out, "dp", axis=0, tiled=True),
    )
    full_project = jnp.concatenate([full_query, full_key, full_value], axis=1)
    rows_all = lax.all_gather(inputs, "tensor", axis=0, tiled=True)
    projected = jnp.dot(rows_all, full_project, preferred_element_type=jnp.float32).astype(
        jnp.bfloat16
    )
    query = projected[:, :columns]
    kv_local = projected[:, columns:]
    everything = lax.all_gather(kv_local, "dp", axis=0, tiled=True)
    tree_kv = lax.dynamic_slice_in_dim(everything, tree_index * tree_len, tree_len, 0)
    seg_tree = lax.dynamic_slice_in_dim(token_segment, tree_index * tree_len, tree_len, 0)
    seg_rows = lax.dynamic_slice_in_dim(seg_tree, query_start, group_rows, 0)
    parents = lax.dynamic_slice_in_dim(segment_parent, tree_index, 1, 0)[0]
    labels = jnp.arange(parents.shape[0], dtype=jnp.int32)
    parent_one = jnp.sum(
        jnp.where(seg_rows[:, None] == labels[None, :], parents[None, :], 0), axis=1
    )
    parent_two = jnp.sum(
        jnp.where(parent_one[:, None] == labels[None, :], parents[None, :], 0), axis=1
    )
    allowed = (
        (seg_tree[None, :] == seg_rows[:, None])
        | (seg_tree[None, :] == parent_one[:, None])
        | (seg_tree[None, :] == parent_two[:, None])
    )[:, None, :]
    query_heads = query.reshape(group_rows, local_heads, head_dim)
    forward_all = attend_forward(tree_len, local_heads, head_dim, score_scale)
    forward_operands = (query_heads, tree_kv, prev_logits, allowed)
    mixed, logits, log_total = forward_all(forward_operands)
    attended = lax.psum_scatter(
        jnp.dot(mixed, full_attn, preferred_element_type=jnp.float32).astype(jnp.bfloat16),
        "tensor",
        scatter_dimension=0,
        tiled=True,
    ).astype(jnp.float32)
    first_sum = inputs.astype(jnp.float32) + attended
    hidden, norm_one_back = jax.vjp(layer_norm, first_sum, norm1_gain, norm1_shift)
    hidden_all = lax.all_gather(hidden.astype(jnp.bfloat16), "tensor", axis=0, tiled=True)
    inner_raw = jnp.dot(
        hidden_all, full_inner, preferred_element_type=jnp.float32
    ) + full_bias.astype(jnp.float32)
    active, gelu_back = jax.vjp(gelu_exact, inner_raw)
    active_low = active.astype(jnp.bfloat16)
    ffn_out = lax.psum_scatter(
        jnp.dot(active_low, full_outer, preferred_element_type=jnp.float32).astype(jnp.bfloat16),
        "tensor",
        scatter_dimension=0,
        tiled=True,
    ).astype(jnp.float32)
    result, norm_two_back = jax.vjp(layer_norm, hidden + ffn_out, norm2_gain, norm2_shift)
    grad_second, grad_gain_two, grad_shift_two = norm_two_back(out_grad.astype(jnp.float32))
    grad_rows_all = lax.all_gather(grad_second.astype(jnp.bfloat16), "tensor", axis=0, tiled=True)
    grad_active = jnp.dot(grad_rows_all, full_outer.T, preferred_element_type=jnp.float32).astype(
        jnp.bfloat16
    )
    grad_w_outer = jnp.dot(active_low.T, grad_rows_all, preferred_element_type=jnp.float32)
    (grad_inner,) = gelu_back(grad_active.astype(jnp.float32))
    grad_inner_low = grad_inner.astype(jnp.bfloat16)
    grad_bias = jnp.sum(grad_inner_low.astype(jnp.float32), axis=0)
    grad_w_inner = jnp.dot(hidden_all.T, grad_inner_low, preferred_element_type=jnp.float32)
    grad_hidden = grad_second + lax.psum_scatter(
        jnp.dot(grad_inner_low, full_inner.T, preferred_element_type=jnp.float32).astype(
            jnp.bfloat16
        ),
        "tensor",
        scatter_dimension=0,
        tiled=True,
    ).astype(jnp.float32)
    grad_first, grad_gain_one, grad_shift_one = norm_one_back(grad_hidden)
    grad_attn_all = lax.all_gather(grad_first.astype(jnp.bfloat16), "tensor", axis=0, tiled=True)
    grad_mixed = jnp.dot(grad_attn_all, full_attn.T, preferred_element_type=jnp.float32).astype(
        jnp.bfloat16
    )
    grad_w_attn = jnp.dot(mixed.T, grad_attn_all, preferred_element_type=jnp.float32)
    grad_mixed_heads = grad_mixed.reshape(group_rows, local_heads, head_dim)
    backward_all = attend_backward(tree_len, local_heads, head_dim, score_scale)
    backward_operands = (
        query_heads,
        tree_kv,
        prev_logits,
        allowed,
        log_total,
        grad_mixed_heads,
        logit_grad,
    )
    grad_scores, grad_query, tree_grads = backward_all(backward_operands)
    placed = lax.dynamic_update_slice_in_dim(
        jnp.zeros((lax.axis_size("dp") * group_rows, 2 * columns), jnp.float32),
        tree_grads,
        tree_index * tree_len,
        0,
    )
    own_grads = lax.psum_scatter(placed, "dp", scatter_dimension=0, tiled=True)
    grad_project = jnp.concatenate([grad_query, own_grads.astype(jnp.bfloat16)], axis=1)
    grad_w_project = jnp.dot(rows_all.T, grad_project, preferred_element_type=jnp.float32)
    grad_inputs = grad_first + lax.psum_scatter(
        jnp.dot(grad_project, full_project.T, preferred_element_type=jnp.float32).astype(
            jnp.bfloat16
        ),
        "tensor",
        scatter_dimension=0,
        tiled=True,
    ).astype(jnp.float32)
    weight_grads = (
        lax.psum_scatter(grad_w_project[:, :columns], "dp", scatter_dimension=0, tiled=True),
        lax.psum_scatter(
            grad_w_project[:, columns : 2 * columns], "dp", scatter_dimension=0, tiled=True
        ),
        lax.psum_scatter(grad_w_project[:, 2 * columns :], "dp", scatter_dimension=0, tiled=True),
        lax.psum_scatter(grad_w_attn, "dp", scatter_dimension=1, tiled=True),
        lax.psum_scatter(grad_w_inner, "dp", scatter_dimension=0, tiled=True),
        lax.psum_scatter(grad_bias, "dp", scatter_dimension=0, tiled=True),
        lax.psum_scatter(grad_w_outer, "dp", scatter_dimension=0, tiled=True),
    )
    norm_grads = lax.psum(
        (grad_gain_one, grad_shift_one, grad_gain_two, grad_shift_two), ("dp", "tensor")
    )
    return (
        result.astype(jnp.bfloat16),
        logits,
        grad_inputs,
        grad_scores,
        weight_grads[0],
        weight_grads[1],
        weight_grads[2],
        weight_grads[3],
        weight_grads[4],
        weight_grads[5],
        weight_grads[6],
        norm_grads[0],
        norm_grads[1],
        norm_grads[2],
        norm_grads[3],
    )


def solution(mesh):
    placed = (
        P(("dp", "tensor"), None),
        P("dp", "tensor", None),
        P("dp", "tensor"),
        P("dp", "tensor"),
        P("dp", "tensor"),
        P("tensor", "dp"),
        P("dp", "tensor"),
        P(("tensor", "dp")),
        P(("tensor", "dp"), None),
        P(),
        P(),
        P(),
        P(),
        P(),
        P(),
        P(("dp", "tensor"), None),
        P("dp", "tensor", None),
    )
    return jax.shard_map(
        shards,
        mesh=mesh,
        in_specs=placed,
        out_specs=(
            P(("dp", "tensor"), None),
            P("dp", "tensor", None),
            P(("dp", "tensor"), None),
            P("dp", "tensor", None),
            P("dp", "tensor"),
            P("dp", "tensor"),
            P("dp", "tensor"),
            P("tensor", "dp"),
            P("dp", "tensor"),
            P(("tensor", "dp")),
            P(("tensor", "dp"), None),
            P(),
            P(),
            P(),
            P(),
        ),
        check_vma=False,
    )
```

profile of v0, /device:TPU:0, one launch (start us, length us, event | category | flops | bytes accessed | tf_op | source)
XLA Modules:
  0.0 1029.3 jit_solution(4397699468486531703)
XLA Ops:
  7.2 33.0 %all_gather.36 = bf16[768,192]{1,0:T(8,128)(2,1)S(1)} all-gather(bf16[96,192]{1,0:T(8,128)(2,1)} %param.19), channel_id=1, replica_groups=mesh['dp'=8,'tensor'=4] {'dp'}, dimensions={0}, use_global_device_ids=true | all-gather | bytes 331776 | tf_op jit(solution)/shard_map/all_gather | solution.py:128
  40.2 31.4 %all_gather.37 = bf16[768,192]{1,0:T(8,128)(2,1)S(1)} all-gather(bf16[96,192]{1,0:T(8,128)(2,1)} %param.20), channel_id=1, replica_groups=mesh['dp'=8,'tensor'=4] {'dp'}, dimensions={0}, use_global_device_ids=true | all-gather | bytes 331776 | tf_op jit(solution)/shard_map/all_gather | solution.py:129
  71.6 31.2 %all_gather.38 = bf16[768,192]{1,0:T(8,128)(2,1)S(1)} all-gather(bf16[96,192]{1,0:T(8,128)(2,1)} %param.21), channel_id=1, replica_groups=mesh['dp'=8,'tensor'=4] {'dp'}, dimensions={0}, use_global_device_ids=true | all-gather | bytes 331776 | tf_op jit(solution)/shard_map/all_gather | solution.py:130
  113.6 16.6 %copy.55 = bf16[512,3,4096]{0,2,1:T(8,128)(2,1)} copy(bf16[512,3,4096]{2,0,1:T(8,128)(2,1)} %param.18) | data formatting | bytes 25165824 | tf_op args[1]
  130.5 32.3 %all_gather.41 = bf16[192,768]{0,1:T(8,128)(2,1)S(1)} all-gather(bf16[192,96]{0,1:T(8,128)(2,1)S(1)} %copy.57), channel_id=1, replica_groups=mesh['dp'=8,'tensor'=4] {'dp'}, dimensions={1}, use_global_device_ids=true | all-gather | bytes 331776 | tf_op jit(solution)/shard_map/all_gather | solution.py:131
  166.3 14.6 %all-gather.4.cloned.1.call-done = bf16[4096,384]{0,1:T(8,128)(2,1)} async-done(((bf16[512,384]{0,1:T(8,128)(2,1)}), bf16[4096,384]{0,1:T(8,128)(2,1)}) %all-gather.4.cloned.1.call-update) | async-done | bytes 3145744 | tf_op jit(solution)/shard_map/all_gather | solution.py:143
  183.4 14.6 %select_reduce_fusion = (f32[512,3]{0,1:T(4,128)S(1)}, f32[512,3,4096]{0,2,1:T(8,128)}) fusion(pred[512,4096]{0,1:T(8,128)(4,1)S(1)} %copy-done, bf16[512,3,4096]{0,2,1:T(8,128)(2,1)} %copy.55, bf16[4096,3,64]{0,2,1:T(8,128)(2,1)S(1)} %bitcast.77, bf16[512,3,64]{0,2,1:T(8,128)(2,1)S(1)} %bitcast.85), kind=kOutput, calls=%fused_computation.13 | convolution fusion | flops 836762112 | bytes 41621504 | tf_op jit(solution)/shard_map/qhe,khe->qhk/dot_general | solution.py:28
  225.4 17.8 %all-reduce = bf16[768]{0:T(1024)(128)(2,1)S(1)} all-reduce(bf16[768]{0:T(1024)(128)(2,1)S(1)} %dynamic-update-slice), channel_id=1, replica_groups=mesh['dp'=8,'tensor'=4] {'dp'}, use_global_device_ids=true, to_apply=%add | all-reduce | flops 768 | bytes 3072
  255.8 31.5 %all-gather.6.cloned.1.call-done = bf16[768,768]{1,0:T(8,128)(2,1)} async-done(((bf16[96,768]{1,0:T(8,128)(2,1)}), bf16[768,768]{1,0:T(8,128)(2,1)}) %all-gather.6.cloned.1.call-update) | async-done | bytes 1179664 | tf_op jit(solution)/shard_map/all_gather | solution.py:132
  293.8 35.6 %all-gather.8.cloned.1.call-done = bf16[768,768]{1,0:T(8,128)(2,1)} async-done(((bf16[96,768]{1,0:T(8,128)(2,1)}), bf16[768,768]{1,0:T(8,128)(2,1)}) %all-gather.8.cloned.1.call-update) | async-done | bytes 1179664 | tf_op jit(solution)/shard_map/all_gather | solution.py:134
  332.8 22.1 %reduce-scatter.22.cloned.1.call-done = bf16[128,768]{1,0:T(8,128)(2,1)} async-done(((bf16[512,768]{1,0:T(8,128)(2,1)}), bf16[128,768]{1,0:T(8,128)(2,1)}) %reduce-scatter.22.cloned.1.call-update) | async-done | bytes 196624 | tf_op jit(solution)/shard_map/reduce_scatter | solution.py:178
  370.4 16.6 %copy.58 = bf16[512,3,4096]{0,2,1:T(8,128)(2,1)} copy(bf16[512,3,4096]{2,0,1:T(8,128)(2,1)} %param.33) | data formatting | bytes 25165824 | tf_op args[16]
  420.0 38.9 %fusion.4 = bf16[512,3,4096]{0,2,1:T(8,128)(2,1)} fusion(bf16[512,3,4096]{0,2,1:T(8,128)(2,1)} %copy.58, f32[512,3,4096]{0,2,1:T(8,128)} %get-tuple-element.87, f32[512,3]{0,1:T(4,128)} %log_add_fusion, pred[512,4096]{0,1:T(8,128)(4,1)} %compare_or_fusion, bf16[4096,3,64]{0,2,1:T(8,128)(2,1)} %bitcast.84, bf16[512,3,64]{0,2,1:T(8,128)(2,1)} %bitcast.90), kind=kOutput, calls=%fused_computation.6 | convolution fusion | flops 1679824384 | bytes 54204416 | tf_op jit(solution)/shard_map/sub | solution.py:70
  480.2 109.5 %reduce-scatter.26.cloned.1.call-done = f32[512,384]{0,1:T(8,128)} async-done(((f32[4096,384]{0,1:T(8,128)}), f32[512,384]{0,1:T(8,128)}) %reduce-scatter.26.cloned.1.call-update) | async-done | bytes 786448 | tf_op jit(solution)/shard_map/reduce_scatter | solution.py:227
  606.1 14.9 %select_convert_fusion = bf16[512,3,4096]{0,2,1:T(8,128)(2,1)} fusion(f32[512,3,4096]{0,2,1:T(8,128)} %get-tuple-element.87, pred[512,4096]{0,1:T(8,128)(4,1)S(1)} %copy-done.2), kind=kLoop, calls=%fused_computation.9 | loop fusion | flops 6291456 | bytes 39845888 | tf_op jit(solution)/shard_map/convert_element_type | solution.py:31
  621.1 16.9 %copy.62 = bf16[512,3,4096]{2,0,1:T(8,128)(2,1)} copy(bf16[512,3,4096]{0,2,1:T(8,128)(2,1)} %select_convert_fusion) | data formatting | bytes 25165824
  638.0 19.7 %all-reduce.1 = f32[768]{0:T(1024)S(1)} all-reduce(f32[768]{0:T(1024)S(1)} %copy-done.34), channel_id=12, replica_groups=mesh['dp'=8,'tensor'=4] {'dp'}, use_global_device_ids=true, to_apply=%region_24.25.clone | all-reduce | flops 768 | bytes 6144
  658.3 16.9 %copy.63 = bf16[512,3,4096]{2,0,1:T(8,128)(2,1)} copy(bf16[512,3,4096]{0,2,1:T(8,128)(2,1)} %fusion.4) | data formatting | bytes 25165824
  675.2 38.2 %all-reduce.2 = (f32[768]{0:T(1024)}, f32[768]{0:T(1024)}, f32[768]{0:T(1024)}, f32[768]{0:T(1024)}) all-reduce(f32[768]{0:T(1024)S(1)} %get-tuple-element.60, f32[768]{0:T(1024)S(1)} %copy-done.28, f32[768]{0:T(1024)S(1)} %get-tuple-element.62, f32[768]{0:T(1024)S(1)} %get-tuple-element.65), channel_id=1, replica_groups=mesh['dp'=8,'tensor'=4] {'dp','tensor'}, use_global_device_ids=true, to_apply=%region_27.28 | all-reduce | flops 3072 | bytes 24576 | tf_op jit(solution)/shard_map/psum | solution.py:249
  716.9 36.8 %reduce-scatter.32.cloned.1.call-done = f32[96,768]{1,0:T(8,128)} async-done(((f32[768,768]{1,0:T(8,128)}), f32[96,768]{1,0:T(8,128)}) %reduce-scatter.32.cloned.1.call-update) | async-done | bytes 294928 | tf_op jit(solution)/shard_map/reduce_scatter | solution.py:247
  753.7 72.6 %reduce-scatter.30.cloned.1.call-done = f32[96,768]{1,0:T(8,128)} async-done(((f32[768,768]{1,0:T(8,128)}), f32[96,768]{1,0:T(8,128)}) %reduce-scatter.30.cloned.1.call-update) | async-done | bytes 294928 | tf_op jit(solution)/shard_map/reduce_scatter | solution.py:245
  826.3 65.6 %reduce-scatter.38.cloned.1.call-done = f32[96,192]{1,0:T(8,128)} async-done(((f32[768,192]{1,0:T(8,128)}), f32[96,192]{1,0:T(8,128)}) %reduce-scatter.38.cloned.1.call-update) | async-done | bytes 73744
  891.9 65.3 %reduce-scatter.36.cloned.1.call-done = f32[96,192]{1,0:T(8,128)} async-done(((f32[768,192]{1,0:T(8,128)}), f32[96,192]{1,0:T(8,128)}) %reduce-scatter.36.cloned.1.call-update) | async-done | bytes 73744
  957.1 65.4 %reduce-scatter.34.cloned.1.call-done = f32[96,192]{1,0:T(8,128)} async-done(((f32[768,192]{1,0:T(8,128)}), f32[96,192]{1,0:T(8,128)}) %reduce-scatter.34.cloned.1.call-update) | async-done | bytes 73744
  (182 shorter events, 155.2 us)
Async XLA Ops:
  7.2 173.7 %all-gather.4.cloned.1.call-start = ((), (), s32[]{:S(2)}) async-start(), calls=%async_computation.11 | async-start | bytes 3538944 | tf_op jit(solution)/shard_map/all_gather | solution.py:143
  40.2 72.4 %copy-start.19 = (bf16[768,192]{1,0:T(8,128)(2,1)}, bf16[768,192]{1,0:T(8,128)(2,1)S(1)}, u32[]{:S(2)}) copy-start(bf16[768,192]{1,0:T(8,128)(2,1)S(1)} %all_gather.36) | copy-start | bytes 884740
  71.6 41.0 %copy-start.20 = (bf16[768,192]{1,0:T(8,128)(2,1)}, bf16[768,192]{1,0:T(8,128)(2,1)S(1)}, u32[]{:S(2)}) copy-start(bf16[768,192]{1,0:T(8,128)(2,1)S(1)} %all_gather.37) | copy-start | bytes 884740
  113.4 130.4 %reduce-scatter.20.cloned.1.call-start = ((), (), s32[]{:S(2)}) async-start(), calls=%async_computation.12 | async-start | bytes 983040 | tf_op jit(solution)/shard_map/reduce_scatter | solution.py:164
  113.5 69.7 %copy-start.14 = (bf16[512,192]{0,1:T(8,128)(2,1)}, bf16[512,192]{0,1:T(8,128)(2,1)S(1)}, u32[]{:S(2)}) copy-start(bf16[512,192]{0,1:T(8,128)(2,1)S(1)} %slice.33) | copy-start | bytes 589828
  162.8 57.8 %copy-start.5 = (bf16[192,768]{0,1:T(8,128)(2,1)}, bf16[192,768]{0,1:T(8,128)(2,1)S(1)}, u32[]{:S(2)}) copy-start(bf16[192,768]{0,1:T(8,128)(2,1)S(1)} %all_gather.41) | copy-start | bytes 884740
  183.2 25.8 %copy-start.13 = (bf16[4096,192]{0,1:T(8,128)(2,1)}, bf16[4096,192]{0,1:T(8,128)(2,1)S(1)}, u32[]{:S(2)}) copy-start(bf16[4096,192]{0,1:T(8,128)(2,1)S(1)} %get-tuple-element.79) | copy-start | bytes 4718596
  222.5 64.8 %all-gather.6.cloned.1.call-start = ((), (), s32[]{:S(2)}) async-start(), calls=%async_computation.13 | async-start | bytes 1327104 | tf_op jit(solution)/shard_map/all_gather | solution.py:132
  223.2 106.2 %all-gather.8.cloned.1.call-start = ((), (), s32[]{:S(2)}) async-start(), calls=%async_computation.14 | async-start | bytes 1327104 | tf_op jit(solution)/shard_map/all_gather | solution.py:134
  223.8 131.1 %reduce-scatter.22.cloned.1.call-start = ((), (), s32[]{:S(2)}) async-start(), calls=%async_computation.15 | async-start | bytes 983040 | tf_op jit(solution)/shard_map/reduce_scatter | solution.py:178
  244.8 149.3 %copy-start.29 = (f32[128]{0:T(128)}, f32[128]{0:T(128)S(1)}, u32[]{:S(2)}) copy-start(f32[128]{0:T(128)S(1)} %broadcast_multiply_fusion.1) | copy-start | bytes 1540
  246.0 148.1 %copy-start.30 = (f32[128]{0:T(128)}, f32[128]{0:T(128)S(1)}, u32[]{:S(2)}) copy-start(f32[128]{0:T(128)S(1)} %fusion.39) | copy-start | bytes 1540
  329.4 25.5 %copy-start.4 = (bf16[128,768]{1,0:T(8,128)(2,1)S(1)}, bf16[128,768]{1,0:T(8,128)(2,1)}, u32[]{:S(2)}) copy-start(bf16[128,768]{1,0:T(8,128)(2,1)} %reduce-scatter.20.cloned.1.call-done) | copy-start | bytes 589828
  332.7 61.4 %reduce-scatter.24.cloned.1.call-start = ((), (), s32[]{:S(2)}) async-start(), calls=%async_computation.16 | async-start | bytes 983040 | tf_op jit(solution)/shard_map/reduce_scatter | solution.py:195
  357.6 36.5 %copy-start.32 = (f32[128]{0:T(128)}, f32[128]{0:T(128)S(1)}, u32[]{:S(2)}) copy-start(f32[128]{0:T(128)S(1)} %negate_multiply_fusion.2) | copy-start | bytes 1540
  370.3 219.3 %reduce-scatter.26.cloned.1.call-start = ((), (), s32[]{:S(2)}) async-start(), calls=%async_computation.17 | async-start | bytes 7077888 | tf_op jit(solution)/shard_map/reduce_scatter | solution.py:227
  470.8 242.7 %reduce-scatter.40.cloned.1.call-start = ((), (), s32[]{:S(2)}) async-start(), calls=%async_computation.24 | async-start | bytes 884736
  473.1 242.0 %reduce-scatter.28.cloned.1.call-start = ((), (), s32[]{:S(2)}) async-start(), calls=%async_computation.18 | async-start | bytes 983040 | tf_op jit(solution)/shard_map/reduce_scatter | solution.py:230
  594.2 159.5 %reduce-scatter.32.cloned.1.call-start = ((), (), s32[]{:S(2)}) async-start(), calls=%async_computation.20 | async-start | bytes 2654208 | tf_op jit(solution)/shard_map/reduce_scatter | solution.py:247
  596.5 229.8 %reduce-scatter.30.cloned.1.call-start = ((), (), s32[]{:S(2)}) async-start(), calls=%async_computation.19 | async-start | bytes 2654208 | tf_op jit(solution)/shard_map/reduce_scatter | solution.py:245
  599.8 292.0 %reduce-scatter.38.cloned.1.call-start = ((), (), s32[]{:S(2)}) async-start(), calls=%async_computation.23 | async-start | bytes 884736
  602.9 354.3 %reduce-scatter.36.cloned.1.call-start = ((), (), s32[]{:S(2)}) async-start(), calls=%async_computation.22 | async-start | bytes 884736
  604.1 418.4 %reduce-scatter.34.cloned.1.call-start = ((), (), s32[]{:S(2)}) async-start(), calls=%async_computation.21 | async-start | bytes 884736
  658.3 56.8 %copy-start.36 = (f32[128]{0:T(128)S(1)}, f32[128]{0:T(128)}, u32[]{:S(2)}) copy-start(f32[128]{0:T(128)} %copy-done.35) | copy-start | bytes 1540
  (34 other events, 342.6 us)
Sparse Core Ops, SparseCore 0:
  113.5 67.3 all-gather.3
  222.6 21.1 reduce-scatter.19
  246.2 41.0 all-gather.5
  289.6 39.8 all-gather.7
  332.9 21.9 reduce-scatter.21
  370.4 23.6 reduce-scatter.23
  470.9 118.7 reduce-scatter.25
  593.3 61.5 reduce-scatter.39
  657.5 22.2 reduce-scatter.27
  684.1 69.5 reduce-scatter.31
  758.2 68.0 reduce-scatter.29
  830.4 61.4 reduce-scatter.37
  895.7 61.3 reduce-scatter.35
  961.2 61.2 reduce-scatter.33
where the time goes:
time: 1040 us; the launch traced here: 1030 us
  waiting for transfers between devices  527 us (51%)
  blocking collectives  238 us (23%)
  matrix products  120 us (12%)
  local copies, waits for them, and re-layouts  81.7 us (8%)
  other arithmetic  45.5 us (4%)
  between operations  16.1 us (2%)
    unnamed x18, waiting for transfers between devices  198 us
    reduce_scatter x1, waiting for transfers between devices, shards(): own_grads = lax.psum_scatter(placed, 'dp', scatter_dimension=0, tiled=True)  109 us
    unnamed x101, local copies, waits for them, and re-layouts  78.4 us
    reduce_scatter x1, waiting for transfers between devices, shards(): lax.psum_scatter(grad_w_inner, 'dp', scatter_dimension=0, tiled=True)  72.6 us
    sub x1, matrix products, run(): grad_weight - jnp.sum(attention_weight * grad_weight, axis=-1, keepdims=T...  38.9 us
    psum x1, blocking collectives, shards(): lax.psum((grad_gain_one, grad_shift_one, grad_gain_two, grad_shift_two),...  38.2 us
    unnamed x2, blocking collectives  37.5 us
    reduce_scatter x1, waiting for transfers between devices, shards(): lax.psum_scatter(grad_w_outer, 'dp', scatter_dimension=0, tiled=True)  36.8 us
  transfers between devices with their start and end apart: 14, of which 12 were waited for; matrix products, arithmetic and copies ran while one was open for 12% of the time, Pallas kernels for 0%

commit v1 on v0

--- a/solution.py
+++ b/solution.py
@@ -247,7 +247,7 @@
         lax.psum_scatter(grad_w_outer, "dp", scatter_dimension=0, tiled=True),
     )
     norm_grads = lax.psum(
-        (grad_gain_one, grad_shift_one, grad_gain_two, grad_shift_two), ("dp", "tensor")
+        lax.psum((grad_gain_one, grad_shift_one, grad_gain_two, grad_shift_two), "tensor"), "dp"
     )
     return (
         result.astype(jnp.bfloat16),

time: 1040 us -> 1040 us (level)
  blocking collectives: 238 us -> 227 us
  waiting for transfers between devices: 527 us -> 538 us
    psum x1, blocking collectives: 38.2 us -> 10.1 us  [shards(): lax.psum((grad_gain_one, grad_shift_one, grad_gain_two, grad_shift_two),...]
    unnamed x2, blocking collectives: 37.5 us -> 54.8 us
    reduce_scatter x1, waiting for transfers between devices: 36.8 us -> 47.2 us  [shards(): lax.psum_scatter(grad_w_outer, 'dp', scatter_dimension=0, tiled=True)]
where the time goes in v1:
time: 1040 us; the launch traced here: 1030 us
  waiting for transfers between devices  538 us (52%)
  blocking collectives  227 us (22%)
  matrix products  120 us (12%)
  local copies, waits for them, and re-layouts  81.7 us (8%)
  other arithmetic  45.5 us (4%)
  between operations  16.1 us (2%)
    unnamed x18, waiting for transfers between devices  198 us
    reduce_scatter x1, waiting for transfers between devices, shards(): own_grads = lax.psum_scatter(placed, 'dp', scatter_dimension=0, tiled=True)  109 us
    unnamed x101, local copies, waits for them, and re-layouts  78.4 us
    reduce_scatter x1, waiting for transfers between devices, shards(): lax.psum_scatter(grad_w_inner, 'dp', scatter_dimension=0, tiled=True)  72.7 us
    unnamed x2, blocking collectives  54.8 us
    reduce_scatter x1, waiting for transfers between devices, shards(): lax.psum_scatter(grad_w_outer, 'dp', scatter_dimension=0, tiled=True)  47.2 us
    sub x1, matrix products, run(): grad_weight - jnp.sum(attention_weight * grad_weight, axis=-1, keepdims=T...  38.8 us
    all_gather x1, waiting for transfers between devices, shards(): lax.all_gather(w_ffn_out, 'dp', axis=0, tiled=True)  35.6 us
  transfers between devices with their start and end apart: 14, of which 12 were waited for; matrix products, arithmetic and copies ran while one was open for 12% of the time, Pallas kernels for 0%

profile of v1, /device:TPU:0, one launch (start us, length us, event | category | flops | bytes accessed | tf_op | source)
XLA Modules:
  0.0 1029.0 jit_solution(65879327940507813)
XLA Ops:
  7.2 33.0 %all_gather.36 = bf16[768,192]{1,0:T(8,128)(2,1)S(1)} all-gather(bf16[96,192]{1,0:T(8,128)(2,1)} %param.19), channel_id=1, replica_groups=mesh['dp'=8,'tensor'=4] {'dp'}, dimensions={0}, use_global_device_ids=true | all-gather | bytes 331776 | tf_op jit(solution)/shard_map/all_gather | solution.py:128
  40.2 31.4 %all_gather.37 = bf16[768,192]{1,0:T(8,128)(2,1)S(1)} all-gather(bf16[96,192]{1,0:T(8,128)(2,1)} %param.20), channel_id=1, replica_groups=mesh['dp'=8,'tensor'=4] {'dp'}, dimensions={0}, use_global_device_ids=true | all-gather | bytes 331776 | tf_op jit(solution)/shard_map/all_gather | solution.py:129
  71.6 31.2 %all_gather.38 = bf16[768,192]{1,0:T(8,128)(2,1)S(1)} all-gather(bf16[96,192]{1,0:T(8,128)(2,1)} %param.21), channel_id=1, replica_groups=mesh['dp'=8,'tensor'=4] {'dp'}, dimensions={0}, use_global_device_ids=true | all-gather | bytes 331776 | tf_op jit(solution)/shard_map/all_gather | solution.py:130
  113.6 16.6 %copy.55 = bf16[512,3,4096]{0,2,1:T(8,128)(2,1)} copy(bf16[512,3,4096]{2,0,1:T(8,128)(2,1)} %param.18) | data formatting | bytes 25165824 | tf_op args[1]
  130.5 32.3 %all_gather.41 = bf16[192,768]{0,1:T(8,128)(2,1)S(1)} all-gather(bf16[192,96]{0,1:T(8,128)(2,1)S(1)} %copy.57), channel_id=1, replica_groups=mesh['dp'=8,'tensor'=4] {'dp'}, dimensions={1}, use_global_device_ids=true | all-gather | bytes 331776 | tf_op jit(solution)/shard_map/all_gather | solution.py:131
  166.3 14.6 %all-gather.4.cloned.1.call-done = bf16[4096,384]{0,1:T(8,128)(2,1)} async-done(((bf16[512,384]{0,1:T(8,128)(2,1)}), bf16[4096,384]{0,1:T(8,128)(2,1)}) %all-gather.4.cloned.1.call-update) | async-done | bytes 3145744 | tf_op jit(solution)/shard_map/all_gather | solution.py:143
  183.4 14.6 %select_reduce_fusion = (f32[512,3]{0,1:T(4,128)S(1)}, f32[512,3,4096]{0,2,1:T(8,128)}) fusion(pred[512,4096]{0,1:T(8,128)(4,1)S(1)} %copy-done, bf16[512,3,4096]{0,2,1:T(8,128)(2,1)} %copy.55, bf16[4096,3,64]{0,2,1:T(8,128)(2,1)S(1)} %bitcast.77, bf16[512,3,64]{0,2,1:T(8,128)(2,1)S(1)} %bitcast.85), kind=kOutput, calls=%fused_computation.13 | convolution fusion | flops 836762112 | bytes 41621504 | tf_op jit(solution)/shard_map/qhe,khe->qhk/dot_general | solution.py:28
  225.4 17.8 %all-reduce = bf16[768]{0:T(1024)(128)(2,1)S(1)} all-reduce(bf16[768]{0:T(1024)(128)(2,1)S(1)} %dynamic-update-slice), channel_id=1, replica_groups=mesh['dp'=8,'tensor'=4] {'dp'}, use_global_device_ids=true, to_apply=%add | all-reduce | flops 768 | bytes 3072
  255.8 31.5 %all-gather.6.cloned.1.call-done = bf16[768,768]{1,0:T(8,128)(2,1)} async-done(((bf16[96,768]{1,0:T(8,128)(2,1)}), bf16[768,768]{1,0:T(8,128)(2,1)}) %all-gather.6.cloned.1.call-update) | async-done | bytes 1179664 | tf_op jit(solution)/shard_map/all_gather | solution.py:132
  293.8 35.6 %all-gather.8.cloned.1.call-done = bf16[768,768]{1,0:T(8,128)(2,1)} async-done(((bf16[96,768]{1,0:T(8,128)(2,1)}), bf16[768,768]{1,0:T(8,128)(2,1)}) %all-gather.8.cloned.1.call-update) | async-done | bytes 1179664 | tf_op jit(solution)/shard_map/all_gather | solution.py:134
  332.8 22.1 %reduce-scatter.22.cloned.1.call-done = bf16[128,768]{1,0:T(8,128)(2,1)} async-done(((bf16[512,768]{1,0:T(8,128)(2,1)}), bf16[128,768]{1,0:T(8,128)(2,1)}) %reduce-scatter.22.cloned.1.call-update) | async-done | bytes 196624 | tf_op jit(solution)/shard_map/reduce_scatter | solution.py:178
  370.4 16.6 %copy.58 = bf16[512,3,4096]{0,2,1:T(8,128)(2,1)} copy(bf16[512,3,4096]{2,0,1:T(8,128)(2,1)} %param.33) | data formatting | bytes 25165824 | tf_op args[16]
  407.0 13.0 %fusion.7 = f32[3,64,4096]{2,1,0:T(8,128)} fusion(bf16[512,3,64]{0,2,1:T(8,128)(2,1)S(1)} %bitcast.89, f32[512,3,4096]{0,2,1:T(8,128)} %get-tuple-element.92, f32[512,3]{0,1:T(4,128)S(1)} %copy-done.31, pred[512,4096]{0,1:T(8,128)(4,1)S(1)} %copy-done.1), kind=kOutput, calls=%fused_computation.15 | convolution fusion | flops 824180736 | bytes 30611456 | tf_op jit(solution)/shard_map/qhk,qhe->khe/dot_general | solution.py:63
  420.0 38.8 %fusion.4 = bf16[512,3,4096]{0,2,1:T(8,128)(2,1)} fusion(bf16[512,3,4096]{0,2,1:T(8,128)(2,1)} %copy.58, f32[512,3,4096]{0,2,1:T(8,128)} %get-tuple-element.92, f32[512,3]{0,1:T(4,128)} %log_add_fusion, pred[512,4096]{0,1:T(8,128)(4,1)} %compare_or_fusion, bf16[4096,3,64]{0,2,1:T(8,128)(2,1)} %bitcast.84, bf16[512,3,64]{0,2,1:T(8,128)(2,1)} %bitcast.90), kind=kOutput, calls=%fused_computation.6 | convolution fusion | flops 1679824384 | bytes 54204416 | tf_op jit(solution)/shard_map/sub | solution.py:70
  480.2 109.5 %reduce-scatter.26.cloned.1.call-done = f32[512,384]{0,1:T(8,128)} async-done(((f32[4096,384]{0,1:T(8,128)}), f32[512,384]{0,1:T(8,128)}) %reduce-scatter.26.cloned.1.call-update) | async-done | bytes 786448 | tf_op jit(solution)/shard_map/reduce_scatter | solution.py:227
  606.1 14.9 %select_convert_fusion = bf16[512,3,4096]{0,2,1:T(8,128)(2,1)} fusion(f32[512,3,4096]{0,2,1:T(8,128)} %get-tuple-element.92, pred[512,4096]{0,1:T(8,128)(4,1)S(1)} %copy-done.2), kind=kLoop, calls=%fused_computation.9 | loop fusion | flops 6291456 | bytes 39845888 | tf_op jit(solution)/shard_map/convert_element_type | solution.py:31
  621.0 16.9 %copy.62 = bf16[512,3,4096]{2,0,1:T(8,128)(2,1)} copy(bf16[512,3,4096]{0,2,1:T(8,128)(2,1)} %select_convert_fusion) | data formatting | bytes 25165824
  637.9 16.9 %copy.63 = bf16[512,3,4096]{2,0,1:T(8,128)(2,1)} copy(bf16[512,3,4096]{0,2,1:T(8,128)(2,1)} %fusion.4) | data formatting | bytes 25165824
  665.0 37.0 %all-reduce.2 = (f32[768]{0:T(1024)S(1)}, f32[768]{0:T(1024)}, f32[768]{0:T(1024)}, f32[768]{0:T(1024)}, f32[768]{0:T(1024)}) all-reduce(f32[768]{0:T(1024)S(1)} %copy-done.34, f32[768]{0:T(1024)S(1)} %get-tuple-element.71, f32[768]{0:T(1024)S(1)} %get-tuple-element.72, ...), channel_id=12, replica_groups=mesh['dp'=8,'tensor'=4] {'dp'}, use_global_device_ids=true, to_apply=%region_24.25.clone | all-reduce | flops 3840 | bytes 30720
  706.0 47.2 %reduce-scatter.32.cloned.1.call-done = f32[96,768]{1,0:T(8,128)} async-done(((f32[768,768]{1,0:T(8,128)}), f32[96,768]{1,0:T(8,128)}) %reduce-scatter.32.cloned.1.call-update) | async-done | bytes 294928 | tf_op jit(solution)/shard_map/reduce_scatter | solution.py:247
  753.3 72.7 %reduce-scatter.30.cloned.1.call-done = f32[96,768]{1,0:T(8,128)} async-done(((f32[768,768]{1,0:T(8,128)}), f32[96,768]{1,0:T(8,128)}) %reduce-scatter.30.cloned.1.call-update) | async-done | bytes 294928 | tf_op jit(solution)/shard_map/reduce_scatter | solution.py:245
  825.9 65.6 %reduce-scatter.38.cloned.1.call-done = f32[96,192]{1,0:T(8,128)} async-done(((f32[768,192]{1,0:T(8,128)}), f32[96,192]{1,0:T(8,128)}) %reduce-scatter.38.cloned.1.call-update) | async-done | bytes 73744
  891.5 65.3 %reduce-scatter.36.cloned.1.call-done = f32[96,192]{1,0:T(8,128)} async-done(((f32[768,192]{1,0:T(8,128)}), f32[96,192]{1,0:T(8,128)}) %reduce-scatter.36.cloned.1.call-update) | async-done | bytes 73744
  956.8 65.5 %reduce-scatter.34.cloned.1.call-done = f32[96,192]{1,0:T(8,128)} async-done(((f32[768,192]{1,0:T(8,128)}), f32[96,192]{1,0:T(8,128)}) %reduce-scatter.34.cloned.1.call-update) | async-done | bytes 73744
  (182 shorter events, 152.3 us)
Async XLA Ops:
  7.2 173.7 %all-gather.4.cloned.1.call-start = ((), (), s32[]{:S(2)}) async-start(), calls=%async_computation.11 | async-start | bytes 3538944 | tf_op jit(solution)/shard_map/all_gather | solution.py:143
  40.2 72.4 %copy-start.19 = (bf16[768,192]{1,0:T(8,128)(2,1)}, bf16[768,192]{1,0:T(8,128)(2,1)S(1)}, u32[]{:S(2)}) copy-start(bf16[768,192]{1,0:T(8,128)(2,1)S(1)} %all_gather.36) | copy-start | bytes 884740
  71.6 41.0 %copy-start.20 = (bf16[768,192]{1,0:T(8,128)(2,1)}, bf16[768,192]{1,0:T(8,128)(2,1)S(1)}, u32[]{:S(2)}) copy-start(bf16[768,192]{1,0:T(8,128)(2,1)S(1)} %all_gather.37) | copy-start | bytes 884740
  113.4 130.4 %reduce-scatter.20.cloned.1.call-start = ((), (), s32[]{:S(2)}) async-start(), calls=%async_computation.12 | async-start | bytes 983040 | tf_op jit(solution)/shard_map/reduce_scatter | solution.py:164
  113.5 69.7 %copy-start.14 = (bf16[512,192]{0,1:T(8,128)(2,1)}, bf16[512,192]{0,1:T(8,128)(2,1)S(1)}, u32[]{:S(2)}) copy-start(bf16[512,192]{0,1:T(8,128)(2,1)S(1)} %slice.33) | copy-start | bytes 589828
  162.8 57.8 %copy-start.5 = (bf16[192,768]{0,1:T(8,128)(2,1)}, bf16[192,768]{0,1:T(8,128)(2,1)S(1)}, u32[]{:S(2)}) copy-start(bf16[192,768]{0,1:T(8,128)(2,1)S(1)} %all_gather.41) | copy-start | bytes 884740
  183.2 25.8 %copy-start.13 = (bf16[4096,192]{0,1:T(8,128)(2,1)}, bf16[4096,192]{0,1:T(8,128)(2,1)S(1)}, u32[]{:S(2)}) copy-start(bf16[4096,192]{0,1:T(8,128)(2,1)S(1)} %get-tuple-element.84) | copy-start | bytes 4718596
  222.5 64.8 %all-gather.6.cloned.1.call-start = ((), (), s32[]{:S(2)}) async-start(), calls=%async_computation.13 | async-start | bytes 1327104 | tf_op jit(solution)/shard_map/all_gather | solution.py:132
  223.2 106.2 %all-gather.8.cloned.1.call-start = ((), (), s32[]{:S(2)}) async-start(), calls=%async_computation.14 | async-start | bytes 1327104 | tf_op jit(solution)/shard_map/all_gather | solution.py:134
  223.8 131.1 %reduce-scatter.22.cloned.1.call-start = ((), (), s32[]{:S(2)}) async-start(), calls=%async_computation.15 | async-start | bytes 983040 | tf_op jit(solution)/shard_map/reduce_scatter | solution.py:178
  244.8 149.3 %copy-start.29 = (f32[128]{0:T(128)}, f32[128]{0:T(128)S(1)}, u32[]{:S(2)}) copy-start(f32[128]{0:T(128)S(1)} %broadcast_multiply_fusion.1) | copy-start | bytes 1540
  246.0 148.1 %copy-start.30 = (f32[128]{0:T(128)}, f32[128]{0:T(128)S(1)}, u32[]{:S(2)}) copy-start(f32[128]{0:T(128)S(1)} %fusion.39) | copy-start | bytes 1540
  332.7 61.4 %reduce-scatter.24.cloned.1.call-start = ((), (), s32[]{:S(2)}) async-start(), calls=%async_computation.16 | async-start | bytes 983040 | tf_op jit(solution)/shard_map/reduce_scatter | solution.py:195
  357.6 36.5 %copy-start.32 = (f32[128]{0:T(128)}, f32[128]{0:T(128)S(1)}, u32[]{:S(2)}) copy-start(f32[128]{0:T(128)S(1)} %negate_multiply_fusion.2) | copy-start | bytes 1540
  370.3 219.3 %reduce-scatter.26.cloned.1.call-start = ((), (), s32[]{:S(2)}) async-start(), calls=%async_computation.17 | async-start | bytes 7077888 | tf_op jit(solution)/shard_map/reduce_scatter | solution.py:227
  470.7 231.9 %reduce-scatter.40.cloned.1.call-start = ((), (), s32[]{:S(2)}) async-start(), calls=%async_computation.24 | async-start | bytes 884736
  473.1 231.2 %reduce-scatter.28.cloned.1.call-start = ((), (), s32[]{:S(2)}) async-start(), calls=%async_computation.18 | async-start | bytes 983040 | tf_op jit(solution)/shard_map/reduce_scatter | solution.py:230
  594.1 159.1 %reduce-scatter.32.cloned.1.call-start = ((), (), s32[]{:S(2)}) async-start(), calls=%async_computation.20 | async-start | bytes 2654208 | tf_op jit(solution)/shard_map/reduce_scatter | solution.py:247
  596.4 229.5 %reduce-scatter.30.cloned.1.call-start = ((), (), s32[]{:S(2)}) async-start(), calls=%async_computation.19 | async-start | bytes 2654208 | tf_op jit(solution)/shard_map/reduce_scatter | solution.py:245
  599.8 291.7 %reduce-scatter.38.cloned.1.call-start = ((), (), s32[]{:S(2)}) async-start(), calls=%async_computation.23 | async-start | bytes 884736
  602.8 353.9 %reduce-scatter.36.cloned.1.call-start = ((), (), s32[]{:S(2)}) async-start(), calls=%async_computation.22 | async-start | bytes 884736
  604.1 418.1 %reduce-scatter.34.cloned.1.call-start = ((), (), s32[]{:S(2)}) async-start(), calls=%async_computation.21 | async-start | bytes 884736
  637.9 27.1 %copy-start.34 = (f32[768]{0:T(1024)S(1)}, f32[768]{0:T(1024)}, u32[]{:S(2)}) copy-start(f32[768]{0:T(1024)} %get-tuple-element.94) | copy-start | bytes 9220
  637.9 66.3 %copy-start.36 = (f32[128]{0:T(128)S(1)}, f32[128]{0:T(128)}, u32[]{:S(2)}) copy-start(f32[128]{0:T(128)} %copy-done.35) | copy-start | bytes 1540
  (34 other events, 351.1 us)
Sparse Core Ops, SparseCore 0:
  113.5 67.3 all-gather.3
  222.6 21.1 reduce-scatter.19
  246.2 41.0 all-gather.5
  289.6 39.8 all-gather.7
  332.8 21.9 reduce-scatter.21
  370.4 23.6 reduce-scatter.23
  470.8 118.7 reduce-scatter.25
  593.3 61.5 reduce-scatter.39
  657.5 22.2 reduce-scatter.27
  684.0 69.1 reduce-scatter.31
  757.7 68.1 reduce-scatter.29
  830.0 61.4 reduce-scatter.37
  895.4 61.3 reduce-scatter.35
  960.9 61.3 reduce-scatter.33
